TPU v7x, 32 devices: a whole 2x2x4 slice. The times are simulated.
32 devices in a mesh: pairs: 2 (over y), pb: 4 (over z), ka: 2 (over core), wa: 2 (over x).
Axes of the slice: x: 2, y: 2, z: 4, core: 2. Of those that a mesh axis runs over, the one named last changes fastest.
Arguments:
- clean_rows: bfloat16 [4096, 8192], P(('pairs', 'pb', 'ka'), 'wa'), parts along dimension 0, may hold values from -72 to 72
- noised_rows: bfloat16 [4096, 8192], P(('pairs', 'pb', 'ka'), 'wa'), parts along dimension 0, may hold values from -6 to 6
- query_weight: bfloat16 [8192, 512], P('wa'), may hold values from -0.0625 to 0.0625
- key_weight: bfloat16 [8192, 128], P('wa'), may hold values from -0.0625 to 0.0625
- value_weight: bfloat16 [8192, 128], P('wa'), may hold values from -0.0625 to 0.0625
- out_grads: bfloat16 [4096, 512], P(('pairs', 'pb', 'ka'), 'wa'), parts along dimension 0, may hold values from -6 to 6
- lookback: int32 [4096], P('pairs'), parts along dimension 0, may hold values from 1 to 2048
Outputs:
- attribution: float32 [4096], P(('pairs', 'pb', 'ka', 'wa')), parts along dimension 0
There are 2 independent parts, one for each index of `pairs`. A program takes and returns all parts, laid end to end along the dimension named above; an argument that names none is the same for every part. Nothing has to cross between parts.
All inputs are finite; a program needn't handle non-finite values.
Results may differ from a plain program's by a relative error of at most 0.01315.
The roundings to bfloat16 on the way count: a program that leaves them out, or rounds other values in their place, can miss the bound.
Values may be sent and summed in bfloat16 or wider, within the bound.
No kernel may reach another device: no remote copies, remote signals or barrier semaphores. Data moves between devices by JAX's collectives and lax.ppermute only.
A program may use at most 64 MiB of HBM per device.

v0:
```python
import math
import jax
import jax.numpy as jnp
from jax import lax
from jax.sharding import PartitionSpec as P

very_low = -1e30


def joined(array, axis, combine):
    everything = jax.tree.map(lambda part: lax.all_gather(part, axis), array)
    first = jax.tree.map(lambda part: part[0], everything)

    def turn(k, so_far):
        return combine(so_far, jax.tree.map(lambda part: part[k], everything))

    return lax.fori_loop(1, lax.axis_size(axis), turn, first)


def split_heads(pair_block, head_size):
    return pair_block.reshape(pair_block.shape[0], pair_block.shape[1] // head_size, head_size)


def visible_pairs(query_pos, query_look, key_pos):
    distance = query_pos[:, None] - key_pos[None, :]
    return (distance >= 0) & (distance < query_look[:, None])


def combine_stats(earlier, later):
    highest = jnp.maximum(earlier[0], later[0])
    left_scale = jnp.exp(earlier[0] - highest)
    right_scale = jnp.exp(later[0] - highest)
    return (
        highest,
        earlier[1] * left_scale + later[1] * right_scale,
        earlier[2] * left_scale + later[2] * right_scale,
    )


def block_stats(
    query_block, grad_block, query_pos, query_look, key_block, value_block, key_pos, score_scale
):
    scores = (
        jnp.einsum("bhd,kd->bhk", query_block, key_block, preferred_element_type=jnp.float32)
        * score_scale
    )
    grad_value = jnp.einsum(
        "bhd,kd->bhk", grad_block, value_block, preferred_element_type=jnp.float32
    )
    visible = visible_pairs(query_pos, query_look, key_pos)[:, None, :]
    masked = jnp.where(visible, scores, very_low)
    highest = jnp.max(masked, axis=2)
    weights = jnp.where(visible, jnp.exp(masked - highest[:, :, None]), 0.0)
    return (highest, jnp.sum(weights, axis=2), jnp.sum(weights * grad_value, axis=2))


def block_changes(
    query_block,
    grad_block,
    query_pos,
    query_look,
    row_parts,
    key_block,
    value_block,
    noised_block,
    key_pos,
    score_scale,
):
    highest, row_total, weighted, mean_now = row_parts
    scores = (
        jnp.einsum("bhd,kd->bhk", query_block, key_block, preferred_element_type=jnp.float32)
        * score_scale
    )
    patched = (
        jnp.einsum("bhd,kd->bhk", query_block, noised_block, preferred_element_type=jnp.float32)
        * score_scale
    )
    grad_value = jnp.einsum(
        "bhd,kd->bhk", grad_block, value_block, preferred_element_type=jnp.float32
    )
    visible = visible_pairs(query_pos, query_look, key_pos)[:, None, :]
    held = highest[:, :, None]
    scores = jnp.where(visible, scores, held)
    patched = jnp.where(visible, patched, held)
    shifted = jnp.maximum(held, patched)
    factor = jnp.exp(held - shifted)
    swapped = jnp.exp(patched - shifted) - jnp.exp(scores - shifted)
    divisor = jnp.maximum(row_total[:, :, None] * factor + swapped, 1.0)
    change = (weighted[:, :, None] * factor + swapped * grad_value) / divisor - mean_now[:, :, None]
    return jnp.sum(jnp.where(visible, change, 0.0), axis=(0, 1))


def tile_stats(pair_piece, query_pos, query_look, key_tile, key_pos, score_scale, head_size):
    row_count = pair_piece.shape[0]
    head_cols = pair_piece.shape[1] // 2
    block_rows = math.gcd(row_count, 512)
    key_count = key_tile.shape[0]
    key_width = math.gcd(key_count, 1024)

    def one_block(block_index):
        offset = block_index * block_rows
        pair_block = lax.dynamic_slice_in_dim(pair_piece, offset, block_rows, 0)
        query_block = split_heads(pair_block[:, :head_cols], head_size)
        grad_block = split_heads(pair_block[:, head_cols:], head_size)
        block_pos = lax.dynamic_slice_in_dim(query_pos, offset, block_rows, 0)
        block_look = lax.dynamic_slice_in_dim(query_look, offset, block_rows, 0)
        head_count = query_block.shape[1]

        def one_key(running, key_index):
            key_offset = key_index * key_width
            key_block = lax.dynamic_slice(key_tile, (key_offset, 0), (key_width, head_size))
            value_block = lax.dynamic_slice(
                key_tile, (key_offset, head_size), (key_width, head_size)
            )
            block_keys = lax.dynamic_slice_in_dim(key_pos, key_offset, key_width, 0)
            block_part = block_stats(
                query_block,
                grad_block,
                block_pos,
                block_look,
                key_block,
                value_block,
                block_keys,
                score_scale,
            )
            return (combine_stats(running, block_part), None)

        empty_rows = jnp.zeros((block_rows, head_count), jnp.float32)
        start_stats = (
            jnp.full((block_rows, head_count), very_low, jnp.float32),
            empty_rows,
            empty_rows,
        )
        result, _ = lax.scan(
            one_key, start_stats, jnp.arange(key_count // key_width, dtype=jnp.int32)
        )
        return result

    if block_rows == row_count:
        return one_block(0)
    stacked = lax.map(one_block, jnp.arange(row_count // block_rows, dtype=jnp.int32))
    return tuple((member.reshape(row_count, member.shape[2]) for member in stacked))


def tile_changes(
    pair_tile, query_pos, query_look, merged_stats, key_tile, key_pos, score_scale, head_size
):
    row_count = pair_tile.shape[0]
    head_cols = pair_tile.shape[1] // 2
    block_rows = math.gcd(row_count, 512)
    key_count = key_tile.shape[0]
    key_width = math.gcd(key_count, 1024)
    highest, row_total, weighted = merged_stats
    row_parts = (highest, row_total, weighted, weighted / row_total)

    def one_block(running, block_index):
        offset = block_index * block_rows
        pair_block = lax.dynamic_slice_in_dim(pair_tile, offset, block_rows, 0)
        query_block = split_heads(pair_block[:, :head_cols], head_size)
        grad_block = split_heads(pair_block[:, head_cols:], head_size)
        block_pos = lax.dynamic_slice_in_dim(query_pos, offset, block_rows, 0)
        block_look = lax.dynamic_slice_in_dim(query_look, offset, block_rows, 0)
        block_rows_stats = tuple(
            (lax.dynamic_slice_in_dim(member, offset, block_rows, 0) for member in row_parts)
        )

        def one_key(key_index):
            key_offset = key_index * key_width
            key_block = lax.dynamic_slice(key_tile, (key_offset, 0), (key_width, head_size))
            value_block = lax.dynamic_slice(
                key_tile, (key_offset, head_size), (key_width, head_size)
            )
            noised_block = lax.dynamic_slice(
                key_tile, (key_offset, 2 * head_size), (key_width, head_size)
            )
            block_keys = lax.dynamic_slice_in_dim(key_pos, key_offset, key_width, 0)
            return block_changes(
                query_block,
                grad_block,
                block_pos,
                block_look,
                block_rows_stats,
                key_block,
                value_block,
                noised_block,
                block_keys,
                score_scale,
            )

        changes = lax.map(one_key, jnp.arange(key_count // key_width, dtype=jnp.int32))
        return (running + changes.reshape(key_count), None)

    summed, _ = lax.scan(
        one_block,
        jnp.zeros((key_count,), jnp.float32),
        jnp.arange(row_count // block_rows, dtype=jnp.int32),
    )
    return summed


def shards(clean_rows, noised_rows, query_weight, key_weight, value_weight, out_grads, lookback):
    head_size = key_weight.shape[1]
    score_scale = 1.0 / math.sqrt(head_size)
    pb_size = lax.axis_size("pb")
    ka_size = lax.axis_size("ka")
    pb_index = lax.axis_index("pb")
    ka_index = lax.axis_index("ka")
    pair_rows = clean_rows.shape[0]
    side_weight = jnp.concatenate([key_weight, value_weight], axis=1)
    query_terms = jnp.dot(clean_rows, query_weight, preferred_element_type=jnp.float32)
    queries = lax.psum_scatter(query_terms, "wa", scatter_dimension=1, tiled=True).astype(
        jnp.bfloat16
    )
    key_side = lax.psum_scatter(
        jnp.concatenate(
            [
                jnp.dot(clean_rows, side_weight, preferred_element_type=jnp.float32),
                jnp.dot(noised_rows, key_weight, preferred_element_type=jnp.float32),
            ],
            axis=1,
        ),
        "wa",
        scatter_dimension=0,
        tiled=True,
    ).astype(jnp.bfloat16)
    pair_data = jnp.concatenate([queries, out_grads], axis=1)
    look_grid = lookback.reshape(pb_size, ka_size, pair_rows)
    tile_base = pb_index * (ka_size * pair_rows)
    key_tile = lax.all_gather(key_side, ("pb", "wa"), axis=0, tiled=True)
    row_ids = jnp.arange(key_tile.shape[0], dtype=jnp.int32)
    key_pos = (
        row_ids // pair_rows * (ka_size * pair_rows) + ka_index * pair_rows + row_ids % pair_rows
    )
    look_tile = lax.dynamic_index_in_dim(look_grid, pb_index, 0, keepdims=False).reshape(-1)
    pair_piece = lax.all_gather(pair_data, "ka", axis=0, tiled=True)
    row_ids = jnp.arange(pair_piece.shape[0], dtype=jnp.int32)
    highest, row_total, weighted, pair_tile = tile_stats(
        pair_piece, tile_base + row_ids, look_tile, key_tile, key_pos, score_scale, head_size
    ) + (pair_piece,)
    merged_stats = joined((highest, row_total, weighted), "ka", combine_stats)
    query_pos = tile_base + jnp.arange(pair_tile.shape[0], dtype=jnp.int32)
    key_part = tile_changes(
        pair_tile, query_pos, look_tile, merged_stats, key_tile, key_pos, score_scale, head_size
    )
    return lax.psum_scatter(key_part, ("pb", "wa"), scatter_dimension=0, tiled=True)


def solution(mesh):
    in_specs = (
        P(("pairs", "pb", "ka"), "wa"),
        P(("pairs", "pb", "ka"), "wa"),
        P("wa", None),
        P("wa", None),
        P("wa", None),
        P(("pairs", "pb", "ka"), "wa"),
        P("pairs"),
    )
    out_specs = P(("pairs", "pb", "ka", "wa"))
    return jax.shard_map(shards, mesh=mesh, in_specs=in_specs, out_specs=out_specs, check_vma=False)
```

profile of v0, /device:TPU:0, one launch (start us, length us, event | category | flops | bytes accessed | tf_op | source)
XLA Modules:
  0.0 103.1 jit_solution(1232725400893335930)
XLA Ops:
  6.5 2.8 %fusion.47 = f32[256,128]{0,1:T(8,128)S(1)} fusion(bf16[256,4096]{1,0:T(8,128)(2,1)} %param.8, bf16[4096,128]{1,0:T(8,128)(2,1)} %param.10), kind=kOutput, calls=%fused_computation.77 | convolution fusion | flops 268435456 | bytes 3276800 | tf_op jit(solution)/shard_map/dot_general | solution.py:218
  9.4 2.3 %fusion.10 = f32[256,256]{0,1:T(8,128)S(1)} fusion(bf16[256,4096]{1,0:T(8,128)(2,1)S(1)} %copy-done, bf16[4096,128]{1,0:T(8,128)(2,1)} %param.11, bf16[4096,128]{1,0:T(8,128)(2,1)} %param.10), kind=kOutput, calls=%fused_computation.19 | convolution fusion | flops 541065216 | bytes 4456448 | tf_op jit(solution)/shard_map/dot_general | solution.py:217
  11.7 0.8 pad_maximum_fusion
  12.5 0.0 reduce-scatter.5.cloned.1.call-update
  12.5 0.0 copy-start.2
  12.5 0.0 copy-start.3
  12.5 0.0 reduce-scatter.3.cloned.1.call-start
  12.6 4.3 %fusion.46 = f32[256,512]{1,0:T(8,128)} fusion(bf16[256,4096]{1,0:T(8,128)(2,1)S(1)} %copy-done, bf16[4096,512]{1,0:T(8,128)(2,1)} %param.9), kind=kOutput, calls=%fused_computation.76 | convolution fusion | flops 1073741824 | bytes 6815744 | tf_op jit(solution)/shard_map/dot_general | solution.py:210
  16.8 0.0 reduce-scatter.3.cloned.1.call-update
  17.0 0.6 dynamic-slice
  18.2 0.6 fusion.9
  18.8 9.7 %reduce-scatter.5.cloned.1.call-done = f32[128,384]{0,1:T(8,128)} async-done(((f32[256,384]{0,1:T(8,128)}), f32[128,384]{0,1:T(8,128)}) %reduce-scatter.5.cloned.1.call-update) | async-done | bytes 196624 | tf_op jit(solution)/shard_map/reduce_scatter | solution.py:214
  28.6 0.9 convert_element_type.7
  29.5 32.1 %all_gather.19 = bf16[1024,384]{0,1:T(8,128)(2,1)S(1)} all-gather(bf16[128,384]{0,1:T(8,128)(2,1)S(1)} %convert_element_type.7), channel_id=1, replica_groups=mesh['pairs'=2,'pb'=4,'ka'=2,'wa'=2] {'pb','wa'}, dimensions={0}, use_global_device_ids=true | all-gather | bytes 884736 | tf_op jit(solution)/shard_map/all_gather | solution.py:229
  61.6 1.0 convert_element_type.6
  62.6 2.2 %all_gather.18 = bf16[512,512]{1,0:T(8,128)(2,1)S(1)} all-gather(bf16[256,512]{1,0:T(8,128)(2,1)S(1)} %pad_maximum_fusion.1), channel_id=1, replica_groups=mesh['pairs'=2,'pb'=4,'ka'=2,'wa'=2] {'ka'}, dimensions={0}, use_global_device_ids=true | all-gather | bytes 786432 | tf_op jit(solution)/shard_map/all_gather | solution.py:235
  64.8 1.1 %select_reduce_fusion.1 = (f32[512,2]{0,1:T(2,128)S(1)}, f32[512,2,1024]{2,0,1:T(8,128)S(1)}) fusion(pred[512,1024]{1,0:T(8,128)(4,1)S(1)} %fusion.9, bf16[1024,384]{0,1:T(8,128)(2,1)S(1)} %all_gather.19, bf16[64,2,8,128]{3,2,1,0:T(8,128)(2,1)S(1)} %get-tuple-element.110), kind=kOutput, calls=%fused_computation.10 | convolution fusion | flops 271580160 | bytes 5246976 | tf_op jit(solution)/shard_map/while/body/eval_jaxpr/bhd,kd->bhk/dot_general | solution.py:44
  65.9 2.0 %fusion.4 = (f32[512,2]{0,1:T(2,128)S(1)}, f32[512,2]{0,1:T(2,128)S(1)}, f32[512,2,1024]{2,0,1:T(8,128)S(1)}) fusion(f32[512,2,1024]{2,0,1:T(8,128)S(1)} %get-tuple-element.116, f32[512,2]{0,1:T(2,128)S(1)} %get-tuple-element.115, pred[512,1024]{1,0:T(8,128)(4,1)S(1)} %fusion.9, bf16[1024,384]{0,1:T(8,128)(2,1)S(1)} %all_gather.19, ...), kind=kOutput, calls=%fused_computation.13 | convolution fusion | flops 275773440 | bytes 9449472 | tf_op jit(solution)/shard_map/while/body/eval_jaxpr/bhd,kd->bhk/dot_general | solution.py:47
  67.9 1.8 %all_gather.20 = f32[2,512,2]{1,2,0:T(2,128)S(1)} all-gather(f32[1,512,2]{1,2,0:T(2,128)S(1)} %get-tuple-element.112), channel_id=1, replica_groups=mesh['pairs'=2,'pb'=4,'ka'=2,'wa'=2] {'ka'}, dimensions={0}, use_global_device_ids=true | all-gather | bytes 12288 | tf_op jit(solution)/shard_map/all_gather | solution.py:11
  69.7 1.8 %all_gather.21 = f32[2,512,2]{1,2,0:T(2,128)S(1)} all-gather(f32[1,512,2]{1,2,0:T(2,128)S(1)} %get-tuple-element.114), channel_id=1, replica_groups=mesh['pairs'=2,'pb'=4,'ka'=2,'wa'=2] {'ka'}, dimensions={0}, use_global_device_ids=true | all-gather | bytes 12288 | tf_op jit(solution)/shard_map/all_gather | solution.py:11
  71.5 1.8 %all_gather.22 = f32[2,512,2]{1,2,0:T(2,128)S(1)} all-gather(f32[1,512,2]{1,2,0:T(2,128)S(1)} %get-tuple-element.113), channel_id=1, replica_groups=mesh['pairs'=2,'pb'=4,'ka'=2,'wa'=2] {'ka'}, dimensions={0}, use_global_device_ids=true | all-gather | bytes 12288 | tf_op jit(solution)/shard_map/all_gather | solution.py:11
  73.4 4.5 %select_reduce_fusion = f32[1024]{0:T(1024)S(1)} fusion(f32[512,2,1024]{2,0,1:T(8,128)S(1)} %get-tuple-element.117, f32[512,2,1024]{2,0,1:T(8,128)S(1)} %get-tuple-element.116, f32[512,2]{0,1:T(2,128)S(1)} %get-tuple-element.94, f32[512,2]{0,1:T(2,128)S(1)} %get-tuple-element.107, f32[512,2]{0,1:T(2,128)S(1)} %get-tuple-element.109, ...), kind=kOutput, calls=%fused_computation.7 | convolution fusion | flops 288357376 | bytes 9457664 | tf_op jit(solution)/shard_map/while/body/eval_jaxpr/while/body/eval_jaxpr/bhd,kd->bhk/dot_general | solution.py:75
  77.9 17.8 %all-reduce = f32[1024]{0:T(1024)S(1)} all-reduce(f32[1024]{0:T(1024)S(1)} %select_reduce_fusion), channel_id=4, replica_groups=mesh['pairs'=2,'pb'=4,'ka'=2,'wa'=2] {'pb','wa'}, use_global_device_ids=true, to_apply=%region_6.7.clone | all-reduce | flops 1024 | bytes 8192
  95.7 0.6 dynamic-slice.1
  (17 shorter events, 0.2 us)
Async XLA Ops:
  6.5 2.8 %copy-start = (bf16[256,4096]{1,0:T(8,128)(2,1)S(1)}, bf16[256,4096]{1,0:T(8,128)(2,1)}, u32[]{:S(2)}) copy-start(bf16[256,4096]{1,0:T(8,128)(2,1)} %param.7) | copy-start | bytes 6291460
  6.5 22.0 %reduce-scatter.5.cloned.1.call-start = ((), (), s32[]{:S(2)}) async-start(), calls=%async_computation.3 | async-start | bytes 589824 | tf_op jit(solution)/shard_map/reduce_scatter | solution.py:214
  12.5 4.4 %copy-start.2 = (s32[2048]{0:T(1024)S(1)}, s32[2048]{0:T(1024)}, u32[]{:S(2)}) copy-start(s32[2048]{0:T(1024)} %param.13) | copy-start | bytes 24580
  12.5 4.4 %copy-start.3 = (u32[32]{0:T(128)S(1)}, u32[32]{0:T(128)}, u32[]{:S(2)}) copy-start(u32[32]{0:T(128)} %constant.133) | copy-start | bytes 388
  12.5 50.0 %copy-start.1 = (bf16[256,256]{1,0:T(8,128)(2,1)S(1)}, bf16[256,256]{1,0:T(8,128)(2,1)}, u32[]{:S(2)}) copy-start(bf16[256,256]{1,0:T(8,128)(2,1)} %param.12) | copy-start | bytes 393220
  12.5 49.1 %reduce-scatter.3.cloned.1.call-start = ((), (), s32[]{:S(2)}) async-start(), calls=%async_computation.2 | async-start | bytes 786432 | tf_op jit(solution)/shard_map/reduce_scatter | solution.py:211
Sparse Core Ops, SparseCore 0:
  12.6 15.8 reduce-scatter.4
  30.8 22.4 reduce-scatter.2
where the time goes:
time: 103 us
  blocking collectives  57.5 us (56%)
  matrix products  17 us (17%)
  between operations  14.2 us (14%)
  waiting for transfers between devices  9.76 us (9%)
  other arithmetic  3.36 us (3%)
  local copies, waits for them, and re-layouts  1.25 us (1%)
    all_gather x1, blocking collectives, shards(): key_tile = lax.all_gather(key_side, ('pb', 'wa'), axis=0, tiled=True)  32.1 us
    unnamed x1, blocking collectives  17.8 us
    reduce_scatter x1, waiting for transfers between devices, shards(): lax.psum_scatter(jnp.concatenate([jnp.dot(clean_rows, side_weight, prefer...  9.73 us
    all_gather x3, blocking collectives, joined(): everything = jax.tree.map(lambda part: lax.all_gather(part, axis), array)  5.44 us
    dot_general x1, matrix products, block_changes(): jnp.einsum('bhd,kd->bhk', query_block, noised_block, preferred_element_ty...  4.54 us
    dot_general x1, matrix products, shards(): jnp.dot(clean_rows, query_weight, preferred_element_type=jnp.float32)  4.25 us
    dot_general x1, matrix products, shards(): jnp.dot(noised_rows, key_weight, preferred_element_type=jnp.float32)  2.83 us
    dot_general x1, matrix products, shards(): jnp.dot(clean_rows, side_weight, preferred_element_type=jnp.float32)  2.3 us
  transfers between devices with their start and end apart: 2, of which 1 were waited for; matrix products, arithmetic and copies ran while one was open for 6% of the time, Pallas kernels for 0%

commit v1 on v0

--- a/solution.py
+++ b/solution.py
@@ -5,6 +5,23 @@
 from jax.sharding import PartitionSpec as P
 
 very_low = -1e30
+
+
+def laid_out(blocks, dim):
+    shape = list(blocks.shape[1:])
+    shape[dim] *= blocks.shape[0]
+    return jnp.moveaxis(blocks, 0, dim).reshape(shape)
+
+
+def ring_gather(x, axis, dim):
+    count = lax.axis_size(axis)
+    upward = [(i, (i + 1) % count) for i in range(count)]
+    pieces = [x]
+    while len(pieces) < count:
+        pieces.append(lax.ppermute(pieces[-1], axis, upward))
+    index = lax.axis_index(axis)
+    pieces = jnp.stack(pieces)[(index - jnp.arange(count)) % count]
+    return laid_out(pieces, dim)
 
 
 def joined(array, axis, combine):
@@ -226,7 +243,7 @@
     pair_data = jnp.concatenate([queries, out_grads], axis=1)
     look_grid = lookback.reshape(pb_size, ka_size, pair_rows)
     tile_base = pb_index * (ka_size * pair_rows)
-    key_tile = lax.all_gather(key_side, ("pb", "wa"), axis=0, tiled=True)
+    key_tile = ring_gather(key_side, ("pb", "wa"), 0)
     row_ids = jnp.arange(key_tile.shape[0], dtype=jnp.int32)
     key_pos = (
         row_ids // pair_rows * (ka_size * pair_rows) + ka_index * pair_rows + row_ids % pair_rows

time: 103 us -> 124 us (1.20)
  waiting for transfers between devices: 9.76 us -> 52.6 us
  blocking collectives: 57.5 us -> 24.8 us
  local copies, waits for them, and re-layouts: 1.25 us -> 9.55 us
  matrix products: 17 us -> 18.3 us
    ppermute x0 -> x7, waiting for transfers between devices: none -> 40.8 us  [ring_gather(): pieces.append(lax.ppermute(pieces[-1], axis, upward))]
    all_gather x1 -> x0, blocking collectives: 32.1 us -> none  [shards(): key_tile = lax.all_gather(key_side, ('pb', 'wa'), axis=0, tiled=True)]
    unnamed x13 -> x25, local copies, waits for them, and re-layouts: 1.24 us -> 5.89 us
    gather x0 -> x2, local copies, waits for them, and re-layouts: none -> 3.01 us  [ring_gather(): pieces = jnp.stack(pieces)[(index - jnp.arange(count)) % count]]
    reduce_scatter x1, waiting for transfers between devices: 0.01 us -> 2.04 us  [shards(): lax.psum_scatter(query_terms, 'wa', scatter_dimension=1, tiled=True)]
    unnamed x0 -> x1, other arithmetic: none -> 1.58 us
  transfers between devices with their start and end apart: 2 -> 9, of which waited for: 1 -> 9; matrix products, arithmetic and copies ran while one was open for 6% -> 10% of each run, Pallas kernels for 0% -> 0%
where the time goes in v1:
time: 124 us
  waiting for transfers between devices  52.6 us (42%)
  blocking collectives  24.8 us (20%)
  matrix products  18.3 us (15%)
  between operations  14.3 us (12%)
  local copies, waits for them, and re-layouts  9.55 us (8%)
  other arithmetic  4 us (3%)
    ppermute x7, waiting for transfers between devices, ring_gather(): pieces.append(lax.ppermute(pieces[-1], axis, upward))  40.8 us
    unnamed x1, blocking collectives  17.1 us
    reduce_scatter x1, waiting for transfers between devices, shards(): lax.psum_scatter(jnp.concatenate([jnp.dot(clean_rows, side_weight, prefer...  9.71 us
    unnamed x25, local copies, waits for them, and re-layouts  5.89 us
    all_gather x3, blocking collectives, joined(): everything = jax.tree.map(lambda part: lax.all_gather(part, axis), array)  5.44 us
    dot_general x1, matrix products, block_changes(): jnp.einsum('bhd,kd->bhk', query_block, noised_block, preferred_element_ty...  4.67 us
    dot_general x1, matrix products, shards(): jnp.dot(clean_rows, query_weight, preferred_element_type=jnp.float32)  4.25 us
    gather x2, local copies, waits for them, and re-layouts, ring_gather(): pieces = jnp.stack(pieces)[(index - jnp.arange(count)) % count]  3.01 us
  transfers between devices with their start and end apart: 9, of which 9 were waited for; matrix products, arithmetic and copies ran while one was open for 10% of the time, Pallas kernels for 0%

profile of v1, /device:TPU:0, one launch (start us, length us, event | category | flops | bytes accessed | tf_op | source)
XLA Modules:
  0.0 124.1 jit_solution(5941340598718557580)
XLA Ops:
  6.5 2.8 %fusion.49 = f32[256,128]{0,1:T(8,128)S(1)} fusion(bf16[256,4096]{1,0:T(8,128)(2,1)} %param.8, bf16[4096,128]{1,0:T(8,128)(2,1)} %param.10), kind=kOutput, calls=%fused_computation.93 | convolution fusion | flops 268435456 | bytes 3276800 | tf_op jit(solution)/shard_map/dot_general | solution.py:235
  9.4 2.3 %fusion.10 = f32[256,256]{0,1:T(8,128)S(1)} fusion(bf16[256,4096]{1,0:T(8,128)(2,1)S(1)} %copy-done, bf16[4096,128]{1,0:T(8,128)(2,1)} %param.11, bf16[4096,128]{1,0:T(8,128)(2,1)} %param.10), kind=kOutput, calls=%fused_computation.20 | convolution fusion | flops 541065216 | bytes 4456448 | tf_op jit(solution)/shard_map/dot_general | solution.py:234
  12.6 4.3 %fusion.48 = f32[256,512]{1,0:T(8,128)} fusion(bf16[256,4096]{1,0:T(8,128)(2,1)S(1)} %copy-done, bf16[4096,512]{1,0:T(8,128)(2,1)} %param.9), kind=kOutput, calls=%fused_computation.92 | convolution fusion | flops 1073741824 | bytes 6815744 | tf_op jit(solution)/shard_map/dot_general | solution.py:227
  18.8 9.7 %reduce-scatter.5.cloned.1.call-done = f32[128,384]{0,1:T(8,128)} async-done(((f32[256,384]{0,1:T(8,128)}), f32[128,384]{0,1:T(8,128)}) %reduce-scatter.5.cloned.1.call-update) | async-done | bytes 196624 | tf_op jit(solution)/shard_map/reduce_scatter | solution.py:231
  28.5 1.6 %bitcast_dynamic-update-slice_fusion.7 = (bf16[8,128,384]{1,2,0:T(8,128)(2,1)}, bf16[128,384]{0,1:T(8,128)(2,1)S(1)}) fusion(f32[128,384]{0,1:T(8,128)} %reduce-scatter.5.cloned.1.call-done), kind=kLoop, calls=%fused_computation.43 | loop fusion | flops 49151 | bytes 393216
  30.5 7.0 %collective-permute-done = bf16[128,384]{0,1:T(8,128)(2,1)S(1)} collective-permute-done((bf16[128,384]{0,1:T(8,128)(2,1)S(1)}, bf16[128,384]{0,1:T(8,128)(2,1)S(1)}, u32[]{:S(2)}, u32[]{:S(2)}) %collective-permute-start) | collective-permute-done | bytes 98336 | tf_op jit(solution)/shard_map/ppermute | solution.py:21
  38.1 6.8 %collective-permute-done.1 = bf16[128,384]{0,1:T(8,128)(2,1)S(1)} collective-permute-done((bf16[128,384]{0,1:T(8,128)(2,1)S(1)}, bf16[128,384]{0,1:T(8,128)(2,1)S(1)}, u32[]{:S(2)}, u32[]{:S(2)}) %collective-permute-start.1) | collective-permute-done | bytes 98336 | tf_op jit(solution)/shard_map/ppermute | solution.py:21
  45.5 2.0 %reduce-scatter.3.cloned.1.call-done = f32[256,256]{1,0:T(8,128)} async-done(((f32[256,512]{1,0:T(8,128)}), f32[256,256]{1,0:T(8,128)}) %reduce-scatter.3.cloned.1.call-update) | async-done | bytes 262160 | tf_op jit(solution)/shard_map/reduce_scatter | solution.py:228
  47.6 1.0 convert_element_type.6
  48.6 2.2 %all_gather.15 = bf16[512,512]{1,0:T(8,128)(2,1)S(1)} all-gather(bf16[256,512]{1,0:T(8,128)(2,1)S(1)} %pad_maximum_fusion.1), channel_id=1, replica_groups=mesh['pairs'=2,'pb'=4,'ka'=2,'wa'=2] {'ka'}, dimensions={0}, use_global_device_ids=true | all-gather | bytes 786432 | tf_op jit(solution)/shard_map/all_gather | solution.py:252
  50.7 0.8 slice_bitcast_fusion.7
  53.0 6.5 %collective-permute-done.3 = bf16[128,384]{0,1:T(8,128)(2,1)S(1)} collective-permute-done((bf16[128,384]{0,1:T(8,128)(2,1)S(1)}, bf16[128,384]{0,1:T(8,128)(2,1)S(1)}, u32[]{:S(2)}, u32[]{:S(2)}) %collective-permute-start.3) | collective-permute-done | bytes 98336 | tf_op jit(solution)/shard_map/ppermute | solution.py:21
  60.1 6.7 %collective-permute-done.4 = bf16[128,384]{0,1:T(8,128)(2,1)S(1)} collective-permute-done((bf16[128,384]{0,1:T(8,128)(2,1)S(1)}, bf16[128,384]{0,1:T(8,128)(2,1)S(1)}, u32[]{:S(2)}, u32[]{:S(2)}) %collective-permute-start.4) | collective-permute-done | bytes 98336 | tf_op jit(solution)/shard_map/ppermute | solution.py:21
  67.4 6.7 %collective-permute-done.5 = bf16[128,384]{0,1:T(8,128)(2,1)S(1)} collective-permute-done((bf16[128,384]{0,1:T(8,128)(2,1)S(1)}, bf16[128,384]{0,1:T(8,128)(2,1)S(1)}, u32[]{:S(2)}, u32[]{:S(2)}) %collective-permute-start.5) | collective-permute-done | bytes 98336 | tf_op jit(solution)/shard_map/ppermute | solution.py:21
  74.7 6.7 %collective-permute-done.6 = bf16[128,384]{0,1:T(8,128)(2,1)S(1)} collective-permute-done((bf16[128,384]{0,1:T(8,128)(2,1)S(1)}, bf16[128,384]{0,1:T(8,128)(2,1)S(1)}, u32[]{:S(2)}, u32[]{:S(2)}) %collective-permute-start.6) | collective-permute-done | bytes 98336 | tf_op jit(solution)/shard_map/ppermute | solution.py:21
  82.1 1.8 %gather_fusion = bf16[8,128,384]{1,2,0:T(8,128)(2,1)S(1)} fusion(bf16[8,128,384]{1,2,0:T(8,128)(2,1)} %bitcast_dynamic-update-slice_fusion, s32[1024]{0:T(1024)S(1)} %pad_clamp_fusion), kind=kCustom, calls=%fused_computation | custom fusion | bytes 1572896 | tf_op jit(solution)/shard_map/gather | solution.py:23
  83.9 1.2 copy.15
  85.1 2.2 %select_reduce_fusion.1 = (f32[512,2]{0,1:T(2,128)S(1)}, f32[512,2,1024]{2,0,1:T(8,128)S(1)}) fusion(pred[512,1024]{1,0:T(8,128)(4,1)S(1)} %fusion.9, bf16[1024,384]{1,0:T(8,128)(2,1)} %bitcast.134, bf16[64,2,8,128]{3,2,1,0:T(8,128)(2,1)} %get-tuple-element.112), kind=kOutput, calls=%fused_computation.11 | convolution fusion | flops 271580160 | bytes 5246976 | tf_op jit(solution)/shard_map/while/body/eval_jaxpr/bhd,kd->bhk/dot_general | solution.py:61
  87.3 2.1 %fusion.4 = (f32[512,2]{0,1:T(2,128)S(1)}, f32[512,2]{0,1:T(2,128)S(1)}, f32[512,2,1024]{2,0,1:T(8,128)S(1)}) fusion(f32[512,2,1024]{2,0,1:T(8,128)S(1)} %get-tuple-element.118, f32[512,2]{0,1:T(2,128)S(1)} %get-tuple-element.117, pred[512,1024]{1,0:T(8,128)(4,1)S(1)} %fusion.9, bf16[1024,384]{1,0:T(8,128)(2,1)S(1)} %bitcast.135, ...), kind=kOutput, calls=%fused_computation.14 | convolution fusion | flops 275773440 | bytes 9449472 | tf_op jit(solution)/shard_map/while/body/eval_jaxpr/bhd,kd->bhk/dot_general | solution.py:64
  89.4 1.8 %all_gather.16 = f32[2,512,2]{1,2,0:T(2,128)S(1)} all-gather(f32[1,512,2]{1,2,0:T(2,128)S(1)} %get-tuple-element.114), channel_id=1, replica_groups=mesh['pairs'=2,'pb'=4,'ka'=2,'wa'=2] {'ka'}, dimensions={0}, use_global_device_ids=true | all-gather | bytes 12288 | tf_op jit(solution)/shard_map/all_gather | solution.py:28
  91.2 1.8 %all_gather.17 = f32[2,512,2]{1,2,0:T(2,128)S(1)} all-gather(f32[1,512,2]{1,2,0:T(2,128)S(1)} %get-tuple-element.116), channel_id=1, replica_groups=mesh['pairs'=2,'pb'=4,'ka'=2,'wa'=2] {'ka'}, dimensions={0}, use_global_device_ids=true | all-gather | bytes 12288 | tf_op jit(solution)/shard_map/all_gather | solution.py:28
  93.1 1.8 %all_gather.18 = f32[2,512,2]{1,2,0:T(2,128)S(1)} all-gather(f32[1,512,2]{1,2,0:T(2,128)S(1)} %get-tuple-element.115), channel_id=1, replica_groups=mesh['pairs'=2,'pb'=4,'ka'=2,'wa'=2] {'ka'}, dimensions={0}, use_global_device_ids=true | all-gather | bytes 12288 | tf_op jit(solution)/shard_map/all_gather | solution.py:28
  94.9 4.7 %select_reduce_fusion = f32[1024]{0:T(1024)S(1)} fusion(f32[512,2,1024]{2,0,1:T(8,128)S(1)} %get-tuple-element.142, f32[512,2,1024]{2,0,1:T(8,128)S(1)} %get-tuple-element.118, f32[512,2]{0,1:T(2,128)S(1)} %get-tuple-element.94, f32[512,2]{0,1:T(2,128)S(1)} %get-tuple-element.107, f32[512,2]{0,1:T(2,128)S(1)} %get-tuple-element.109, ...), kind=kOutput, calls=%fused_computation.8 | convolution fusion | flops 288357376 | bytes 9457664 | tf_op jit(solution)/shard_map/while/body/eval_jaxpr/while/body/eval_jaxpr/bhd,kd->bhk/dot_general | solution.py:92
  99.6 17.1 %all-reduce = f32[1024]{0:T(1024)S(1)} all-reduce(f32[1024]{0:T(1024)S(1)} %select_reduce_fusion), channel_id=4, replica_groups=mesh['pairs'=2,'pb'=4,'ka'=2,'wa'=2] {'pb','wa'}, use_global_device_ids=true, to_apply=%region_6.7.clone | all-reduce | flops 1024 | bytes 8192
  (47 shorter events, 8.4 us)
Async XLA Ops:
  6.5 2.8 %copy-start = (bf16[256,4096]{1,0:T(8,128)(2,1)S(1)}, bf16[256,4096]{1,0:T(8,128)(2,1)}, u32[]{:S(2)}) copy-start(bf16[256,4096]{1,0:T(8,128)(2,1)} %param.7) | copy-start | bytes 6291460
  6.5 22.0 %reduce-scatter.5.cloned.1.call-start = ((), (), s32[]{:S(2)}) async-start(), calls=%async_computation.3 | async-start | bytes 589824 | tf_op jit(solution)/shard_map/reduce_scatter | solution.py:231
  12.5 4.4 %copy-start.5 = (s32[2048]{0:T(1024)S(1)}, s32[2048]{0:T(1024)}, u32[]{:S(2)}) copy-start(s32[2048]{0:T(1024)} %param.13) | copy-start | bytes 24580
  12.5 4.5 %copy-start.6 = (u32[32]{0:T(128)S(1)}, u32[32]{0:T(128)}, u32[]{:S(2)}) copy-start(u32[32]{0:T(128)} %constant.152) | copy-start | bytes 388
  12.5 36.0 %copy-start.4 = (bf16[256,256]{1,0:T(8,128)(2,1)S(1)}, bf16[256,256]{1,0:T(8,128)(2,1)}, u32[]{:S(2)}) copy-start(bf16[256,256]{1,0:T(8,128)(2,1)} %param.12) | copy-start | bytes 393220
  12.5 35.0 %reduce-scatter.3.cloned.1.call-start = ((), (), s32[]{:S(2)}) async-start(), calls=%async_computation.2 | async-start | bytes 786432 | tf_op jit(solution)/shard_map/reduce_scatter | solution.py:228
  30.1 7.3 %collective-permute-start = (bf16[128,384]{0,1:T(8,128)(2,1)S(1)}, bf16[128,384]{0,1:T(8,128)(2,1)S(1)}, u32[]{:S(2)}, u32[]{:S(2)}) collective-permute-start(bf16[128,384]{0,1:T(8,128)(2,1)S(1)} %get-tuple-element.111), channel_id=1, source_target_pairs={{0,1},{1,4},{4,5},{5,8},{8,9},{9,12},{12,13},{13,0},{2,3},{3,6},{6... | collective-permute-start | bytes 294920 | tf_op jit(solution)/shard_map/ppermute | solution.py:21
  37.4 7.4 %collective-permute-start.1 = (bf16[128,384]{0,1:T(8,128)(2,1)S(1)}, bf16[128,384]{0,1:T(8,128)(2,1)S(1)}, u32[]{:S(2)}, u32[]{:S(2)}) collective-permute-start(bf16[128,384]{0,1:T(8,128)(2,1)S(1)} %collective-permute-done), channel_id=1, source_target_pairs={{0,1},{1,4},{4,5},{5,8},{8,9},{9,12},{12,13},{13,0},{2,3},{3,6},{6... | collective-permute-start | bytes 294920 | tf_op jit(solution)/shard_map/ppermute | solution.py:21
  44.9 7.3 %collective-permute-start.2 = (bf16[128,384]{0,1:T(8,128)(2,1)S(1)}, bf16[128,384]{0,1:T(8,128)(2,1)S(1)}, u32[]{:S(2)}, u32[]{:S(2)}) collective-permute-start(bf16[128,384]{0,1:T(8,128)(2,1)S(1)} %collective-permute-done.1), channel_id=1, source_target_pairs={{0,1},{1,4},{4,5},{5,8},{8,9},{9,12},{12,13},{13,0},{2,3},{3,6},{6... | collective-permute-start | bytes 294920 | tf_op jit(solution)/shard_map/ppermute | solution.py:21
  52.2 7.3 %collective-permute-start.3 = (bf16[128,384]{0,1:T(8,128)(2,1)S(1)}, bf16[128,384]{0,1:T(8,128)(2,1)S(1)}, u32[]{:S(2)}, u32[]{:S(2)}) collective-permute-start(bf16[128,384]{0,1:T(8,128)(2,1)S(1)} %collective-permute-done.2), channel_id=1, source_target_pairs={{0,1},{1,4},{4,5},{5,8},{8,9},{9,12},{12,13},{13,0},{2,3},{3,6},{6... | collective-permute-start | bytes 294920 | tf_op jit(solution)/shard_map/ppermute | solution.py:21
  59.5 7.3 %collective-permute-start.4 = (bf16[128,384]{0,1:T(8,128)(2,1)S(1)}, bf16[128,384]{0,1:T(8,128)(2,1)S(1)}, u32[]{:S(2)}, u32[]{:S(2)}) collective-permute-start(bf16[128,384]{0,1:T(8,128)(2,1)S(1)} %collective-permute-done.3), channel_id=1, source_target_pairs={{0,1},{1,4},{4,5},{5,8},{8,9},{9,12},{12,13},{13,0},{2,3},{3,6},{6... | collective-permute-start | bytes 294920 | tf_op jit(solution)/shard_map/ppermute | solution.py:21
  66.8 7.3 %collective-permute-start.5 = (bf16[128,384]{0,1:T(8,128)(2,1)S(1)}, bf16[128,384]{0,1:T(8,128)(2,1)S(1)}, u32[]{:S(2)}, u32[]{:S(2)}) collective-permute-start(bf16[128,384]{0,1:T(8,128)(2,1)S(1)} %collective-permute-done.4), channel_id=1, source_target_pairs={{0,1},{1,4},{4,5},{5,8},{8,9},{9,12},{12,13},{13,0},{2,3},{3,6},{6... | collective-permute-start | bytes 294920 | tf_op jit(solution)/shard_map/ppermute | solution.py:21
  74.1 7.3 %collective-permute-start.6 = (bf16[128,384]{0,1:T(8,128)(2,1)S(1)}, bf16[128,384]{0,1:T(8,128)(2,1)S(1)}, u32[]{:S(2)}, u32[]{:S(2)}) collective-permute-start(bf16[128,384]{0,1:T(8,128)(2,1)S(1)} %collective-permute-done.5), channel_id=1, source_target_pairs={{0,1},{1,4},{4,5},{5,8},{8,9},{9,12},{12,13},{13,0},{2,3},{3,6},{6... | collective-permute-start | bytes 294920 | tf_op jit(solution)/shard_map/ppermute | solution.py:21
  85.1 2.2 %copy-start.1 = (bf16[8,128,384]{2,1,0:T(8,128)(2,1)S(1)}, bf16[8,128,384]{2,1,0:T(8,128)(2,1)}, u32[]{:S(2)}) copy-start(bf16[8,128,384]{2,1,0:T(8,128)(2,1)} %copy.15) | copy-start | bytes 2359300
  85.1 2.2 %copy-start.3 = (bf16[64,2,8,128]{3,2,1,0:T(8,128)(2,1)S(1)}, bf16[64,2,8,128]{3,2,1,0:T(8,128)(2,1)}, u32[]{:S(2)}) copy-start(bf16[64,2,8,128]{3,2,1,0:T(8,128)(2,1)} %get-tuple-element.113) | copy-start | bytes 786436
  87.3 7.6 %copy-start.2 = (bf16[64,2,8,128]{3,2,1,0:T(8,128)(2,1)S(1)}, bf16[64,2,8,128]{3,2,1,0:T(8,128)(2,1)}, u32[]{:S(2)}) copy-start(bf16[64,2,8,128]{3,2,1,0:T(8,128)(2,1)} %get-tuple-element.112) | copy-start | bytes 786436
Sparse Core Ops, SparseCore 0:
  12.6 15.8 reduce-scatter.4
  30.8 16.7 reduce-scatter.2
